TPU v7x, 512 devices: a whole 4x4x16 slice. The times are simulated.
512 devices in a mesh: stream: 32 (over z, core), xsec: 16 (over y, x).
Axes of the slice: x: 4, y: 4, z: 16, core: 2. Of those that a mesh axis runs over, the one named last changes fastest.
Arguments:
- right_sides: float32 [32, 2048, 2048], P('stream', None, 'xsec'), may hold values from -6 to 6
- lower_first: bfloat16 [32, 2048, 2048], P('stream', None, 'xsec'), may hold values from -0.0625 to 0.0625
- upper_first: bfloat16 [32, 2048, 2048], P('stream', None, 'xsec'), may hold values from -0.0625 to 0.0625
- lower_second: bfloat16 [32, 2048, 2048], P('stream', None, 'xsec'), may hold values from -0.0625 to 0.0625
- upper_second: bfloat16 [32, 2048, 2048], P('stream', None, 'xsec'), may hold values from -0.0625 to 0.0625
Outputs:
- reduced: float32 [32, 2048, 2048], P('stream', None, 'xsec')
All inputs are finite; a program needn't handle non-finite values.
Results may differ from a plain program's by a relative error of at most 0.0023.
Values may be sent and summed in bfloat16 or wider, within the bound.
No kernel may reach another device: no remote copies, remote signals or barrier semaphores. Data moves between devices by JAX's collectives and lax.ppermute only.
A program may use at most 128 MiB of HBM per device.

v0:
```python
import jax
import jax.numpy as jnp
from jax import lax
from jax.sharding import PartitionSpec as P


def extended(value, sides, width):
    for axis, dim in sides:
        size, length = (lax.axis_size(axis), value.shape[dim])
        up = [(i, (i + 1) % size) for i in range(size - 1)]
        down = [(j, i) for i, j in up]
        last = lax.slice_in_dim(value, length - width, length, axis=dim)
        first = lax.slice_in_dim(value, 0, width, axis=dim)
        before = lax.ppermute(last, axis, up)
        after = lax.ppermute(first, axis, down)
        value = jnp.concatenate([before, value, after], axis=dim)
    return value


def shifted(value, axis, steps):
    count = lax.axis_size(axis)
    first, last = (max(0, -steps), min(count, count - steps))
    return lax.ppermute(value, axis, [(source, source + steps) for source in range(first, last)])


def neighbours_near(outgoing):
    padded = extended(outgoing[None], (("stream", 0),), 1)
    return (padded[0], padded[2])


def neighbours_far(outgoing):
    from_below = shifted(outgoing, "stream", 2)
    from_above = shifted(outgoing, "stream", -2)
    return (from_below, from_above)


def reduce_level(current, lower_blocks, upper_blocks, neighbours):
    outgoing = current.astype(jnp.bfloat16)
    from_below, from_above = neighbours(outgoing)
    lower_piece = lax.all_gather(lower_blocks, "xsec", axis=2, tiled=True)
    upper_piece = lax.all_gather(upper_blocks, "xsec", axis=2, tiled=True)
    total = jnp.dot(lower_piece[0], from_below, preferred_element_type=jnp.float32)
    total = total + jnp.dot(upper_piece[0], from_above, preferred_element_type=jnp.float32)
    return current + total


def on_device(right_sides, lower_first, upper_first, lower_second, upper_second):
    level_one = reduce_level(right_sides[0], lower_first, upper_first, neighbours_near)
    level_two = reduce_level(level_one, lower_second, upper_second, neighbours_far)
    return level_two[None]


def solution(mesh):
    return jax.shard_map(
        on_device,
        mesh=mesh,
        in_specs=(
            P("stream", None, "xsec"),
            P("stream", None, "xsec"),
            P("stream", None, "xsec"),
            P("stream", None, "xsec"),
            P("stream", None, "xsec"),
        ),
        out_specs=P("stream", None, "xsec"),
        check_vma=False,
    )
```

profile of v0, /device:TPU:1, one launch (start us, length us, event | category | flops | bytes accessed | tf_op | source)
XLA Modules:
  0.0 410.1 jit_solution(17927725365922115572)
XLA Ops:
  6.5 0.0 copy-start
  6.5 0.0 all-gather.7.cloned.1.call-start
  6.5 0.7 all-gather.7.cloned.1.call-update
  7.3 0.0 all-gather.5.cloned.1.call-start
  7.3 0.7 all-gather.5.cloned.1.call-update
  8.0 0.0 all-gather.11.cloned.1.call-start
  8.1 0.7 all-gather.11.cloned.1.call-update
  8.7 0.0 all-gather.9.cloned.1.call-start
  8.8 0.5 all-gather.9.cloned.1.call-update
  9.3 1.3 convert_element_type.7
  10.6 8.8 %collective-permute-start.1 = (bf16[1,2048,128]{2,1,0:T(8,128)(2,1)S(1)}, bf16[1,2048,128]{2,1,0:T(8,128)(2,1)}, u32[]{:S(2)}, u32[]{:S(2)}) collective-permute-start(bf16[1,2048,128]{2,1,0:T(8,128)(2,1)S(1)} %convert_element_type.7), channel_id=1, source_target_pairs={{16,0},{32,16},{48,32},{64,48},{80,64},{96,80},{112,96},{128,112},... | collective-permute-start | bytes 1572872 | tf_op jit(solution)/shard_map/ppermute | solution.py:15
  19.4 1.9 collective-permute-start
  21.3 1.2 collective-permute-done.1
  22.5 86.0 %all-gather.7.cloned.1.call-done = bf16[1,2048,2048]{2,1,0:T(8,128)(2,1)} async-done(((bf16[1,2048,128]{2,1,0:T(8,128)(2,1)}), bf16[1,2048,2048]{2,1,0:T(8,128)(2,1)}) %all-gather.7.cloned.1.call-update) | async-done | bytes 8388624 | tf_op jit(solution)/shard_map/all_gather | solution.py:41
  108.5 5.8 %fusion.4 = f32[2048,128]{1,0:T(8,128)S(1)} fusion(bf16[1,2048,2048]{2,1,0:T(8,128)(2,1)} %all-gather.7.cloned.1.call-done, bf16[1,2048,128]{2,1,0:T(8,128)(2,1)} %collective-permute-done.1), kind=kOutput, calls=%fused_computation.4 | convolution fusion | flops 1073741824 | bytes 9961472 | tf_op jit(solution)/shard_map/dot_general | solution.py:43
  114.2 0.0 collective-permute-done
  114.3 0.0 copy-start.1
  114.3 0.8 copy-done.1
  115.1 89.6 %all-gather.5.cloned.1.call-done = bf16[1,2048,2048]{2,1,0:T(8,128)(2,1)} async-done(((bf16[1,2048,128]{2,1,0:T(8,128)(2,1)}), bf16[1,2048,2048]{2,1,0:T(8,128)(2,1)}) %all-gather.5.cloned.1.call-update) | async-done | bytes 8388624 | tf_op jit(solution)/shard_map/all_gather | solution.py:40
  204.6 0.0 copy-done
  204.6 6.6 %fusion.28 = (bf16[2048,128]{1,0:T(8,128)(2,1)}, f32[2048,128]{1,0:T(8,128)S(1)}) fusion(f32[2048,128]{1,0:T(8,128)S(1)} %fusion.4, bf16[1,2048,128]{2,1,0:T(8,128)(2,1)} %copy-done.1, bf16[1,2048,2048]{2,1,0:T(8,128)(2,1)} %all-gather.5.cloned.1.call-done, f32[1,2048,128]{2,1,0:T(8,128)S(1)} %copy-done), kind=kOutput, calls=%fused_computation.16 | convolution fusion | flops 1074528256 | bytes 12582912 | tf_op jit(solution)/shard_map/dot_general | solution.py:42
  211.3 1.3 collective-permute-start.3
  212.6 4.0 collective-permute-start.2
  216.6 84.2 %all-gather.11.cloned.1.call-done = bf16[1,2048,2048]{2,1,0:T(8,128)(2,1)} async-done(((bf16[1,2048,128]{2,1,0:T(8,128)(2,1)}), bf16[1,2048,2048]{2,1,0:T(8,128)(2,1)}) %all-gather.11.cloned.1.call-update) | async-done | bytes 8388624 | tf_op jit(solution)/shard_map/all_gather | solution.py:41
  300.8 0.0 collective-permute-done.3
  300.8 5.7 %fusion = f32[128,2048]{0,1:T(8,128)S(1)} fusion(bf16[2048,128]{1,0:T(8,128)(2,1)S(1)} %collective-permute-done.3, bf16[1,2048,2048]{2,1,0:T(8,128)(2,1)} %all-gather.11.cloned.1.call-done), kind=kOutput, calls=%fused_computation | convolution fusion | flops 1073741824 | bytes 9961472 | tf_op jit(solution)/shard_map/dot_general | solution.py:43
  306.6 90.3 %all-gather.9.cloned.1.call-done = bf16[1,2048,2048]{2,1,0:T(8,128)(2,1)} async-done(((bf16[1,2048,128]{2,1,0:T(8,128)(2,1)}), bf16[1,2048,2048]{2,1,0:T(8,128)(2,1)}) %all-gather.9.cloned.1.call-update) | async-done | bytes 8388624 | tf_op jit(solution)/shard_map/all_gather | solution.py:40
  396.9 0.0 collective-permute-done.2
  396.9 6.7 %fusion.20 = f32[1,2048,128]{2,1,0:T(8,128)} fusion(f32[2048,128]{1,0:T(8,128)S(1)} %get-tuple-element.6, f32[128,2048]{0,1:T(8,128)S(1)} %fusion, bf16[2048,128]{1,0:T(8,128)(2,1)S(1)} %collective-permute-done.2, bf16[1,2048,2048]{2,1,0:T(8,128)(2,1)} %all-gather.9.cloned.1.call-done), kind=kOutput, calls=%fused_computation.12 | convolution fusion | flops 1074266112 | bytes 12058624 | tf_op jit(solution)/shard_map/dot_general | solution.py:42
Async XLA Ops:
  6.5 198.1 %copy-start = (f32[1,2048,128]{2,1,0:T(8,128)S(1)}, f32[1,2048,128]{2,1,0:T(8,128)}, u32[]{:S(2)}) copy-start(f32[1,2048,128]{2,1,0:T(8,128)} %param.5) | copy-start | bytes 3145732
  6.5 101.9 %all-gather.7.cloned.1.call-start = ((), (), s32[]{:S(2)}) async-start(), calls=%async_computation.1 | async-start | bytes 8912896 | tf_op jit(solution)/shard_map/all_gather | solution.py:41
  7.3 197.4 %all-gather.5.cloned.1.call-start = ((), (), s32[]{:S(2)}) async-start(), calls=%async_computation | async-start | bytes 8912896 | tf_op jit(solution)/shard_map/all_gather | solution.py:40
  8.0 292.8 %all-gather.11.cloned.1.call-start = ((), (), s32[]{:S(2)}) async-start(), calls=%async_computation.3 | async-start | bytes 8912896 | tf_op jit(solution)/shard_map/all_gather | solution.py:41
  8.7 388.1 %all-gather.9.cloned.1.call-start = ((), (), s32[]{:S(2)}) async-start(), calls=%async_computation.2 | async-start | bytes 8912896 | tf_op jit(solution)/shard_map/all_gather | solution.py:40
  10.6 11.9 %collective-permute-start.1 = (bf16[1,2048,128]{2,1,0:T(8,128)(2,1)S(1)}, bf16[1,2048,128]{2,1,0:T(8,128)(2,1)}, u32[]{:S(2)}, u32[]{:S(2)}) collective-permute-start(bf16[1,2048,128]{2,1,0:T(8,128)(2,1)S(1)} %convert_element_type.7), channel_id=1, source_target_pairs={{16,0},{32,16},{48,32},{64,48},{80,64},{96,80},{112,96},{128,112},... | collective-permute-start | bytes 1572872 | tf_op jit(solution)/shard_map/ppermute | solution.py:15
  19.4 94.9 %collective-permute-start = (bf16[1,2048,128]{2,1,0:T(8,128)(2,1)S(1)}, bf16[1,2048,128]{2,1,0:T(8,128)(2,1)S(1)}, u32[]{:S(2)}, u32[]{:S(2)}) collective-permute-start(bf16[1,2048,128]{2,1,0:T(8,128)(2,1)S(1)} %convert_element_type.7), channel_id=1, source_target_pairs={{0,16},{16,32},{32,48},{48,64},{64,80},{80,96},{96,112},{112,128},... | collective-permute-start | bytes 1572872 | tf_op jit(solution)/shard_map/ppermute | solution.py:14
  114.3 0.8 copy-start.1
  211.3 89.6 %collective-permute-start.3 = (bf16[2048,128]{1,0:T(8,128)(2,1)}, bf16[2048,128]{1,0:T(8,128)(2,1)S(1)}, u32[]{:S(2)}, u32[]{:S(2)}) collective-permute-start(bf16[2048,128]{1,0:T(8,128)(2,1)} %get-tuple-element.5), channel_id=1, source_target_pairs={{32,0},{48,16},{64,32},{80,48},{96,64},{112,80},{128,96},{144,112}... | collective-permute-start | bytes 1572872 | tf_op jit(solution)/shard_map/ppermute | solution.py:23
  212.6 184.3 %collective-permute-start.2 = (bf16[2048,128]{1,0:T(8,128)(2,1)}, bf16[2048,128]{1,0:T(8,128)(2,1)S(1)}, u32[]{:S(2)}, u32[]{:S(2)}) collective-permute-start(bf16[2048,128]{1,0:T(8,128)(2,1)} %get-tuple-element.5), channel_id=1, source_target_pairs={{0,32},{16,48},{32,64},{48,80},{64,96},{80,112},{96,128},{112,144}... | collective-permute-start | bytes 1572872 | tf_op jit(solution)/shard_map/ppermute | solution.py:23
Sparse Core Ops, SparseCore 0:
  10.3 98.0 all-gather.6
  111.5 93.1 all-gather.4
  207.6 93.1 all-gather.10
  303.7 93.1 all-gather.8
where the time goes:
time: 410 us
  waiting for transfers between devices  354 us (86%)
  matrix products  24.8 us (6%)
  starting transfers between devices  16.1 us (4%)
  between operations  13.2 us (3%)
    all_gather x2, waiting for transfers between devices, reduce_level(): lower_piece = lax.all_gather(lower_blocks, 'xsec', axis=2, tiled=True)  180 us
    all_gather x2, waiting for transfers between devices, reduce_level(): upper_piece = lax.all_gather(upper_blocks, 'xsec', axis=2, tiled=True)  170 us
    dot_general x2, matrix products, reduce_level(): jnp.dot(lower_piece[0], from_below, preferred_element_type=jnp.float32)  13.3 us
    dot_general x2, matrix products, reduce_level(): jnp.dot(upper_piece[0], from_above, preferred_element_type=jnp.float32)  11.5 us
    ppermute x1, starting transfers between devices, extended(): after = lax.ppermute(first, axis, down)  8.79 us
  transfers between devices with their start and end apart: 8, of which 5 were waited for; matrix products, arithmetic and copies ran while one was open for 5% of the time, Pallas kernels for 0%

commit v1 on v0

--- a/solution.py
+++ b/solution.py
@@ -38,7 +38,25 @@
     outgoing = current.astype(jnp.bfloat16)
     from_below, from_above = neighbours(outgoing)
     lower_piece = lax.all_gather(lower_blocks, "xsec", axis=2, tiled=True)
-    upper_piece = lax.all_gather(upper_blocks, "xsec", axis=2, tiled=True)
+    devices, mine, rows = (lax.axis_size("xsec"), lax.axis_index("xsec"), upper_blocks.shape[2])
+    ahead = [(i_2, (i_2 + 1) % devices) for i_2 in range(devices)]
+    left = [(i_2, (i_2 - 1) % devices) for i_2 in range(devices)]
+    upper_piece = jnp.zeros(
+        (*upper_blocks.shape[:2], devices * rows, *upper_blocks.shape[2 + 1 :]), upper_blocks.dtype
+    )
+    upper_piece = lax.dynamic_update_slice_in_dim(upper_piece, upper_blocks, mine * rows, axis=2)
+    from_left = from_right = upper_blocks
+    half = devices // 2
+    for step in range(1, half + 1):
+        from_left = lax.ppermute(from_left, "xsec", ahead)
+        upper_piece = lax.dynamic_update_slice_in_dim(
+            upper_piece, from_left, (mine - step) % devices * rows, axis=2
+        )
+        if step < devices - half:
+            from_right = lax.ppermute(from_right, "xsec", left)
+            upper_piece = lax.dynamic_update_slice_in_dim(
+                upper_piece, from_right, (mine + step) % devices * rows, axis=2
+            )
     total = jnp.dot(lower_piece[0], from_below, preferred_element_type=jnp.float32)
     total = total + jnp.dot(upper_piece[0], from_above, preferred_element_type=jnp.float32)
     return current + total

time: 410 us -> 368 us (0.90)
  waiting for transfers between devices: 354 us -> 176 us
  starting transfers between devices: 16.1 us -> 107 us
  local copies, waits for them, and re-layouts: 0.79 us -> 43.7 us
    all_gather x2 -> x0, waiting for transfers between devices: 170 us -> none  [reduce_level(): upper_piece = lax.all_gather(upper_blocks, 'xsec', axis=2, tiled=True)]
    ppermute x0 -> x30, starting transfers between devices: none -> 90.8 us  [the longest x14 57.6 us: reduce_level(): from_right = lax.ppermute(from_right, 'xsec', left)]
    all_gather x2, waiting for transfers between devices: 180 us -> 118 us  [reduce_level(): lower_piece = lax.all_gather(lower_blocks, 'xsec', axis=2, tiled=True)]
    ppermute x0 -> x30, waiting for transfers between devices: none -> 52.9 us  [the longest x16 51.8 us: reduce_level(): from_left = lax.ppermute(from_left, 'xsec', ahead)]
    dynamic_update_slice x0 -> x32, local copies, waits for them, and re-layouts: none -> 34.2 us  [the longest x16 17.6 us: reduce_level(): lax.dynamic_update_slice_in_dim(upper_piece, from_left, (mine - step) % d...]
    squeeze x0 -> x2, local copies, waits for them, and re-layouts: none -> 8.65 us  [reduce_level(): upper_piece[0]]
    ppermute x2, waiting for transfers between devices: 0.01 us -> 4.56 us  [shifted(): lax.ppermute(value, axis, [(source, source + steps) for source in range(f...]
  transfers between devices with their start and end apart: 8 -> 36, of which waited for: 5 -> 18; matrix products, arithmetic and copies ran while one was open for 5% -> 17% of each run, Pallas kernels for 0% -> 0%
where the time goes in v1:
time: 368 us; the launch traced here: 367 us
  waiting for transfers between devices  176 us (48%)
  starting transfers between devices  107 us (29%)
  local copies, waits for them, and re-layouts  43.7 us (12%)
  matrix products  25.3 us (7%)
  between operations  13.8 us (4%)
    all_gather x2, waiting for transfers between devices, reduce_level(): lower_piece = lax.all_gather(lower_blocks, 'xsec', axis=2, tiled=True)  118 us
    ppermute x14, starting transfers between devices, reduce_level(): from_right = lax.ppermute(from_right, 'xsec', left)  57.6 us
    ppermute x16, waiting for transfers between devices, reduce_level(): from_left = lax.ppermute(from_left, 'xsec', ahead)  51.8 us
    ppermute x16, starting transfers between devices, reduce_level(): from_left = lax.ppermute(from_left, 'xsec', ahead)  33.2 us
    dynamic_update_slice x16, local copies, waits for them, and re-layouts, reduce_level(): lax.dynamic_update_slice_in_dim(upper_piece, from_left, (mine - step) % d...  17.6 us
    dynamic_update_slice x14, local copies, waits for them, and re-layouts, reduce_level(): lax.dynamic_update_slice_in_dim(upper_piece, from_right, (mine + step) %...  14.8 us
    dot_general x2, matrix products, reduce_level(): jnp.dot(lower_piece[0], from_below, preferred_element_type=jnp.float32)  13.3 us
    dot_general x2, matrix products, reduce_level(): jnp.dot(upper_piece[0], from_above, preferred_element_type=jnp.float32)  12 us
  transfers between devices with their start and end apart: 36, of which 18 were waited for; matrix products, arithmetic and copies ran while one was open for 17% of the time, Pallas kernels for 0%

profile of v1, /device:TPU:1, one launch (start us, length us, event | category | flops | bytes accessed | tf_op | source)
XLA Modules:
  0.0 367.0 jit_solution(8707376033500493417)
XLA Ops:
  7.3 4.0 %collective-permute-start.1 = (bf16[1,2048,128]{2,1,0:T(8,128)(2,1)}, bf16[1,2048,128]{2,1,0:T(8,128)(2,1)}, u32[]{:S(2)}, u32[]{:S(2)}) collective-permute-start(bf16[1,2048,128]{2,1,0:T(8,128)(2,1)} %param.7), channel_id=1, source_target_pairs={{0,1},{1,2},{2,3},{3,4},{4,5},{5,6},{6,7},{7,8},{8,9},{9,10},{10,1... | collective-permute-start | bytes 1572872 | tf_op jit(solution)/shard_map/ppermute | solution.py:51
  11.3 5.6 %collective-permute-start.2 = (bf16[1,2048,128]{2,1,0:T(8,128)(2,1)}, bf16[1,2048,128]{2,1,0:T(8,128)(2,1)S(1)}, u32[]{:S(2)}, u32[]{:S(2)}) collective-permute-start(bf16[1,2048,128]{2,1,0:T(8,128)(2,1)} %param.7), channel_id=1, source_target_pairs={{0,15},{1,0},{2,1},{3,2},{4,3},{5,4},{6,5},{7,6},{8,7},{9,8},{10,9... | collective-permute-start | bytes 1572872 | tf_op jit(solution)/shard_map/ppermute | solution.py:56
  18.2 8.4 %collective-permute-start.16 = (bf16[1,2048,128]{2,1,0:T(8,128)(2,1)S(1)}, bf16[1,2048,128]{2,1,0:T(8,128)(2,1)}, u32[]{:S(2)}, u32[]{:S(2)}) collective-permute-start(bf16[1,2048,128]{2,1,0:T(8,128)(2,1)S(1)} %convert_element_type.7), channel_id=1, source_target_pairs={{16,0},{32,16},{48,32},{64,48},{80,64},{96,80},{112,96},{128,112},... | collective-permute-start | bytes 1572872 | tf_op jit(solution)/shard_map/ppermute | solution.py:15
  30.5 4.3 %squeeze.86.clone = bf16[2048,2048]{1,0:T(8,128)(2,1)} broadcast(bf16[]{:T(256)} %constant.151.clone.1), dimensions={} | broadcast | bytes 8388610 | tf_op jit(solution)/shard_map/squeeze | solution.py:61
  35.7 4.3 %squeeze.86.clone.1 = bf16[2048,2048]{1,0:T(8,128)(2,1)} broadcast(bf16[]{:T(256)} %constant.151.clone.1), dimensions={} | broadcast | bytes 8388610 | tf_op jit(solution)/shard_map/squeeze | solution.py:61
  40.9 6.7 %collective-permute-start.19 = (bf16[1,2048,128]{2,1,0:T(8,128)(2,1)S(1)}, bf16[1,2048,128]{2,1,0:T(8,128)(2,1)S(1)}, u32[]{:S(2)}, u32[]{:S(2)}) collective-permute-start(bf16[1,2048,128]{2,1,0:T(8,128)(2,1)S(1)} %copy-done.3), channel_id=1, source_target_pairs={{0,15},{1,0},{2,1},{3,2},{4,3},{5,4},{6,5},{7,6},{8,7},{9,8},{10,9... | collective-permute-start | bytes 1572872 | tf_op jit(solution)/shard_map/ppermute | solution.py:56
  47.6 2.0 bitcast_dynamic-update-slice_fusion.30
  52.4 6.6 %collective-permute-start.4 = (bf16[1,2048,128]{2,1,0:T(8,128)(2,1)S(1)}, bf16[1,2048,128]{2,1,0:T(8,128)(2,1)S(1)}, u32[]{:S(2)}, u32[]{:S(2)}) collective-permute-start(bf16[1,2048,128]{2,1,0:T(8,128)(2,1)S(1)} %collective-permute-done.2), channel_id=1, source_target_pairs={{0,15},{1,0},{2,1},{3,2},{4,3},{5,4},{6,5},{7,6},{8,7},{9,8},{10,9... | collective-permute-start | bytes 1572872 | tf_op jit(solution)/shard_map/ppermute | solution.py:56
  63.7 3.6 collective-permute-done.3
  67.3 3.8 %collective-permute-start.21 = (bf16[1,2048,128]{2,1,0:T(8,128)(2,1)S(1)}, bf16[1,2048,128]{2,1,0:T(8,128)(2,1)S(1)}, u32[]{:S(2)}, u32[]{:S(2)}) collective-permute-start(bf16[1,2048,128]{2,1,0:T(8,128)(2,1)S(1)} %collective-permute-done.19), channel_id=1, source_target_pairs={{0,15},{1,0},{2,1},{3,2},{4,3},{5,4},{6,5},{7,6},{8,7},{9,8},{10,9... | collective-permute-start | bytes 1572872 | tf_op jit(solution)/shard_map/ppermute | solution.py:56
  75.0 3.7 %collective-permute-done.20 = bf16[1,2048,128]{2,1,0:T(8,128)(2,1)S(1)} collective-permute-done((bf16[1,2048,128]{2,1,0:T(8,128)(2,1)S(1)}, bf16[1,2048,128]{2,1,0:T(8,128)(2,1)S(1)}, u32[]{:S(2)}, u32[]{:S(2)}) %collective-permute-start.20) | collective-permute-done | bytes 524320 | tf_op jit(solution)/shard_map/ppermute | solution.py:51
  78.7 3.7 %collective-permute-start.6 = (bf16[1,2048,128]{2,1,0:T(8,128)(2,1)S(1)}, bf16[1,2048,128]{2,1,0:T(8,128)(2,1)S(1)}, u32[]{:S(2)}, u32[]{:S(2)}) collective-permute-start(bf16[1,2048,128]{2,1,0:T(8,128)(2,1)S(1)} %collective-permute-done.4), channel_id=1, source_target_pairs={{0,15},{1,0},{2,1},{3,2},{4,3},{5,4},{6,5},{7,6},{8,7},{9,8},{10,9... | collective-permute-start | bytes 1572872 | tf_op jit(solution)/shard_map/ppermute | solution.py:56
  86.1 3.8 %collective-permute-done.5 = bf16[1,2048,128]{2,1,0:T(8,128)(2,1)S(1)} collective-permute-done((bf16[1,2048,128]{2,1,0:T(8,128)(2,1)S(1)}, bf16[1,2048,128]{2,1,0:T(8,128)(2,1)S(1)}, u32[]{:S(2)}, u32[]{:S(2)}) %collective-permute-start.5) | collective-permute-done | bytes 524320 | tf_op jit(solution)/shard_map/ppermute | solution.py:51
  89.9 3.2 collective-permute-start.23
  94.1 2.0 collective-permute-start.7
  97.0 3.7 %collective-permute-done.22 = bf16[1,2048,128]{2,1,0:T(8,128)(2,1)S(1)} collective-permute-done((bf16[1,2048,128]{2,1,0:T(8,128)(2,1)S(1)}, bf16[1,2048,128]{2,1,0:T(8,128)(2,1)S(1)}, u32[]{:S(2)}, u32[]{:S(2)}) %collective-permute-start.22) | collective-permute-done | bytes 524320 | tf_op jit(solution)/shard_map/ppermute | solution.py:51
  100.7 3.4 collective-permute-start.8
  107.8 3.8 %collective-permute-done.7 = bf16[1,2048,128]{2,1,0:T(8,128)(2,1)S(1)} collective-permute-done((bf16[1,2048,128]{2,1,0:T(8,128)(2,1)S(1)}, bf16[1,2048,128]{2,1,0:T(8,128)(2,1)S(1)}, u32[]{:S(2)}, u32[]{:S(2)}) %collective-permute-start.7) | collective-permute-done | bytes 524320 | tf_op jit(solution)/shard_map/ppermute | solution.py:51
  111.6 3.3 collective-permute-start.25
  115.8 2.0 collective-permute-start.9
  118.7 3.7 %collective-permute-done.24 = bf16[1,2048,128]{2,1,0:T(8,128)(2,1)S(1)} collective-permute-done((bf16[1,2048,128]{2,1,0:T(8,128)(2,1)S(1)}, bf16[1,2048,128]{2,1,0:T(8,128)(2,1)S(1)}, u32[]{:S(2)}, u32[]{:S(2)}) %collective-permute-start.24) | collective-permute-done | bytes 524320 | tf_op jit(solution)/shard_map/ppermute | solution.py:51
  122.4 3.4 collective-permute-start.10
  129.6 3.8 %collective-permute-done.9 = bf16[1,2048,128]{2,1,0:T(8,128)(2,1)S(1)} collective-permute-done((bf16[1,2048,128]{2,1,0:T(8,128)(2,1)S(1)}, bf16[1,2048,128]{2,1,0:T(8,128)(2,1)S(1)}, u32[]{:S(2)}, u32[]{:S(2)}) %collective-permute-start.9) | collective-permute-done | bytes 524320 | tf_op jit(solution)/shard_map/ppermute | solution.py:51
  133.4 3.3 collective-permute-start.27
  137.6 2.0 collective-permute-start.11
  140.5 3.8 %collective-permute-done.26 = bf16[1,2048,128]{2,1,0:T(8,128)(2,1)S(1)} collective-permute-done((bf16[1,2048,128]{2,1,0:T(8,128)(2,1)S(1)}, bf16[1,2048,128]{2,1,0:T(8,128)(2,1)S(1)}, u32[]{:S(2)}, u32[]{:S(2)}) %collective-permute-start.26) | collective-permute-done | bytes 524320 | tf_op jit(solution)/shard_map/ppermute | solution.py:51
  144.2 3.4 collective-permute-start.12
  151.4 3.7 %collective-permute-done.11 = bf16[1,2048,128]{2,1,0:T(8,128)(2,1)S(1)} collective-permute-done((bf16[1,2048,128]{2,1,0:T(8,128)(2,1)S(1)}, bf16[1,2048,128]{2,1,0:T(8,128)(2,1)S(1)}, u32[]{:S(2)}, u32[]{:S(2)}) %collective-permute-start.11) | collective-permute-done | bytes 524320 | tf_op jit(solution)/shard_map/ppermute | solution.py:51
  155.1 3.3 collective-permute-start.29
  162.2 3.8 %collective-permute-done.28 = bf16[1,2048,128]{2,1,0:T(8,128)(2,1)S(1)} collective-permute-done((bf16[1,2048,128]{2,1,0:T(8,128)(2,1)S(1)}, bf16[1,2048,128]{2,1,0:T(8,128)(2,1)S(1)}, u32[]{:S(2)}, u32[]{:S(2)}) %collective-permute-start.28) | collective-permute-done | bytes 524320 | tf_op jit(solution)/shard_map/ppermute | solution.py:51
  166.0 3.4 collective-permute-start.14
  170.3 2.1 collective-permute-start.30
  172.4 2.0 bitcast_dynamic-update-slice_fusion.3
  174.3 2.5 collective-permute-done.13
  176.9 4.5 %collective-permute-start.31 = (bf16[1,2048,128]{2,1,0:T(8,128)(2,1)}, bf16[1,2048,128]{2,1,0:T(8,128)(2,1)}, u32[]{:S(2)}, u32[]{:S(2)}) collective-permute-start(bf16[1,2048,128]{2,1,0:T(8,128)(2,1)} %collective-permute-done.29), channel_id=1, source_target_pairs={{0,15},{1,0},{2,1},{3,2},{4,3},{5,4},{6,5},{7,6},{8,7},{9,8},{10,9... | collective-permute-start | bytes 1572872 | tf_op jit(solution)/shard_map/ppermute | solution.py:56
  182.3 5.5 %collective-permute-done.30 = bf16[1,2048,128]{2,1,0:T(8,128)(2,1)} collective-permute-done((bf16[1,2048,128]{2,1,0:T(8,128)(2,1)S(1)}, bf16[1,2048,128]{2,1,0:T(8,128)(2,1)}, u32[]{:S(2)}, u32[]{:S(2)}) %collective-permute-start.30) | collective-permute-done | bytes 524320 | tf_op jit(solution)/shard_map/ppermute | solution.py:51
  189.7 2.0 bitcast_dynamic-update-slice_fusion.2
  191.6 2.1 collective-permute-start.32
  194.6 6.4 %collective-permute-done.15 = bf16[1,2048,128]{2,1,0:T(8,128)(2,1)S(1)} collective-permute-done((bf16[1,2048,128]{2,1,0:T(8,128)(2,1)S(1)}, bf16[1,2048,128]{2,1,0:T(8,128)(2,1)S(1)}, u32[]{:S(2)}, u32[]{:S(2)}) %collective-permute-start.15) | collective-permute-done | bytes 524320 | tf_op jit(solution)/shard_map/ppermute | solution.py:51
  201.9 5.8 %fusion.22 = f32[2048,128]{1,0:T(8,128)S(1)} fusion(bf16[2048,2048]{1,0:T(8,128)(2,1)} %bitcast_dynamic-update-slice_fusion.16, bf16[1,2048,128]{2,1,0:T(8,128)(2,1)} %collective-permute-done.16), kind=kOutput, calls=%fused_computation.26 | convolution fusion | flops 1073741824 | bytes 9961472 | tf_op jit(solution)/shard_map/dot_general | solution.py:61
  208.5 47.7 %all-gather.3.cloned.1.call-done = bf16[1,2048,2048]{2,1,0:T(8,128)(2,1)} async-done(((bf16[1,2048,128]{2,1,0:T(8,128)(2,1)}), bf16[1,2048,2048]{2,1,0:T(8,128)(2,1)}) %all-gather.3.cloned.1.call-update) | async-done | bytes 8388624 | tf_op jit(solution)/shard_map/all_gather | solution.py:40
  256.2 6.6 %fusion.25 = (bf16[2048,128]{1,0:T(8,128)(2,1)}, f32[2048,128]{1,0:T(8,128)S(1)}) fusion(f32[2048,128]{1,0:T(8,128)S(1)} %fusion.22, bf16[1,2048,128]{2,1,0:T(8,128)(2,1)} %copy-done.1, bf16[1,2048,2048]{2,1,0:T(8,128)(2,1)} %all-gather.3.cloned.1.call-done, f32[1,2048,128]{2,1,0:T(8,128)S(1)} %copy-done), kind=kOutput, calls=%fused_computation.45 | convolution fusion | flops 1074528256 | bytes 12582912 | tf_op jit(solution)/shard_map/dot_general | solution.py:60
  264.2 2.0 bitcast_dynamic-update-slice_fusion.1
  268.1 4.2 %collective-permute-start.17 = (bf16[2048,128]{1,0:T(8,128)(2,1)}, bf16[2048,128]{1,0:T(8,128)(2,1)S(1)}, u32[]{:S(2)}, u32[]{:S(2)}) collective-permute-start(bf16[2048,128]{1,0:T(8,128)(2,1)} %get-tuple-element.5), channel_id=1, source_target_pairs={{0,32},{16,48},{32,64},{48,80},{64,96},{80,112},{96,128},{112,144}... | collective-permute-start | bytes 1572872 | tf_op jit(solution)/shard_map/ppermute | solution.py:23
  272.3 4.6 %collective-permute-done.33 = bf16[2048,128]{1,0:T(8,128)(2,1)S(1)} collective-permute-done((bf16[2048,128]{1,0:T(8,128)(2,1)}, bf16[2048,128]{1,0:T(8,128)(2,1)S(1)}, u32[]{:S(2)}, u32[]{:S(2)}) %collective-permute-start.33) | collective-permute-done | bytes 524320 | tf_op jit(solution)/shard_map/ppermute | solution.py:23
  276.8 6.2 %fusion.26 = f32[2048,128]{1,0:T(8,128)S(1)} fusion(bf16[2048,2048]{1,0:T(8,128)(2,1)} %bitcast_dynamic-update-slice_fusion, bf16[2048,128]{1,0:T(8,128)(2,1)S(1)} %collective-permute-done.33), kind=kOutput, calls=%fused_computation.46 | convolution fusion | flops 1073741824 | bytes 9961472 | tf_op jit(solution)/shard_map/dot_general | solution.py:61
  283.0 70.4 %all-gather.5.cloned.1.call-done = bf16[1,2048,2048]{2,1,0:T(8,128)(2,1)} async-done(((bf16[1,2048,128]{2,1,0:T(8,128)(2,1)}), bf16[1,2048,2048]{2,1,0:T(8,128)(2,1)}) %all-gather.5.cloned.1.call-update) | async-done | bytes 8388624 | tf_op jit(solution)/shard_map/all_gather | solution.py:40
  353.5 6.7 %fusion.19 = f32[1,2048,128]{2,1,0:T(8,128)} fusion(f32[2048,128]{1,0:T(8,128)S(1)} %get-tuple-element.6, f32[2048,128]{1,0:T(8,128)S(1)} %fusion.26, bf16[2048,128]{1,0:T(8,128)(2,1)S(1)} %collective-permute-done.17, bf16[1,2048,2048]{2,1,0:T(8,128)(2,1)} %all-gather.5.cloned.1.call-done), kind=kOutput, calls=%fused_computation.9 | convolution fusion | flops 1074266112 | bytes 12058624 | tf_op jit(solution)/shard_map/dot_general | solution.py:60
  (73 shorter events, 52.6 us)
Async XLA Ops:
  6.5 28.3 %copy-start.2 = (bf16[1,2048,128]{2,1,0:T(8,128)(2,1)S(1)}, bf16[1,2048,128]{2,1,0:T(8,128)(2,1)}, u32[]{:S(2)}) copy-start(bf16[1,2048,128]{2,1,0:T(8,128)(2,1)} %param.7) | copy-start | bytes 1572868
  6.5 249.7 %all-gather.3.cloned.1.call-start = ((), (), s32[]{:S(2)}) async-start(), calls=%async_computation | async-start | bytes 8912896 | tf_op jit(solution)/shard_map/all_gather | solution.py:40
  7.3 346.2 %all-gather.5.cloned.1.call-start = ((), (), s32[]{:S(2)}) async-start(), calls=%async_computation.1 | async-start | bytes 8912896 | tf_op jit(solution)/shard_map/all_gather | solution.py:40
  7.3 33.6 %collective-permute-start.1 = (bf16[1,2048,128]{2,1,0:T(8,128)(2,1)}, bf16[1,2048,128]{2,1,0:T(8,128)(2,1)}, u32[]{:S(2)}, u32[]{:S(2)}) collective-permute-start(bf16[1,2048,128]{2,1,0:T(8,128)(2,1)} %param.7), channel_id=1, source_target_pairs={{0,1},{1,2},{2,3},{3,4},{4,5},{5,6},{6,7},{7,8},{8,9},{9,10},{10,1... | collective-permute-start | bytes 1572872 | tf_op jit(solution)/shard_map/ppermute | solution.py:51
  11.3 38.3 %collective-permute-start.2 = (bf16[1,2048,128]{2,1,0:T(8,128)(2,1)}, bf16[1,2048,128]{2,1,0:T(8,128)(2,1)S(1)}, u32[]{:S(2)}, u32[]{:S(2)}) collective-permute-start(bf16[1,2048,128]{2,1,0:T(8,128)(2,1)} %param.7), channel_id=1, source_target_pairs={{0,15},{1,0},{2,1},{3,2},{4,3},{5,4},{6,5},{7,6},{8,7},{9,8},{10,9... | collective-permute-start | bytes 1572872 | tf_op jit(solution)/shard_map/ppermute | solution.py:56
  18.2 183.7 %collective-permute-start.16 = (bf16[1,2048,128]{2,1,0:T(8,128)(2,1)S(1)}, bf16[1,2048,128]{2,1,0:T(8,128)(2,1)}, u32[]{:S(2)}, u32[]{:S(2)}) collective-permute-start(bf16[1,2048,128]{2,1,0:T(8,128)(2,1)S(1)} %convert_element_type.7), channel_id=1, source_target_pairs={{16,0},{32,16},{48,32},{64,48},{80,64},{96,80},{112,96},{128,112},... | collective-permute-start | bytes 1572872 | tf_op jit(solution)/shard_map/ppermute | solution.py:15
  26.6 181.2 %collective-permute-start = (bf16[1,2048,128]{2,1,0:T(8,128)(2,1)S(1)}, bf16[1,2048,128]{2,1,0:T(8,128)(2,1)S(1)}, u32[]{:S(2)}, u32[]{:S(2)}) collective-permute-start(bf16[1,2048,128]{2,1,0:T(8,128)(2,1)S(1)} %convert_element_type.7), channel_id=1, source_target_pairs={{0,16},{16,32},{32,48},{48,64},{64,80},{80,96},{96,112},{112,128},... | collective-permute-start | bytes 1572872 | tf_op jit(solution)/shard_map/ppermute | solution.py:14
  28.5 23.9 %collective-permute-start.18 = (bf16[1,2048,128]{2,1,0:T(8,128)(2,1)}, bf16[1,2048,128]{2,1,0:T(8,128)(2,1)S(1)}, u32[]{:S(2)}, u32[]{:S(2)}) collective-permute-start(bf16[1,2048,128]{2,1,0:T(8,128)(2,1)} %param.9), channel_id=1, source_target_pairs={{0,1},{1,2},{2,3},{3,4},{4,5},{5,6},{6,7},{7,8},{8,9},{9,10},{10,1... | collective-permute-start | bytes 1572872 | tf_op jit(solution)/shard_map/ppermute | solution.py:51
  30.4 9.5 %copy-start.3 = (bf16[1,2048,128]{2,1,0:T(8,128)(2,1)S(1)}, bf16[1,2048,128]{2,1,0:T(8,128)(2,1)}, u32[]{:S(2)}) copy-start(bf16[1,2048,128]{2,1,0:T(8,128)(2,1)} %param.9) | copy-start | bytes 1572868
  40.9 20.0 %collective-permute-start.19 = (bf16[1,2048,128]{2,1,0:T(8,128)(2,1)S(1)}, bf16[1,2048,128]{2,1,0:T(8,128)(2,1)S(1)}, u32[]{:S(2)}, u32[]{:S(2)}) collective-permute-start(bf16[1,2048,128]{2,1,0:T(8,128)(2,1)S(1)} %copy-done.3), channel_id=1, source_target_pairs={{0,15},{1,0},{2,1},{3,2},{4,3},{5,4},{6,5},{7,6},{8,7},{9,8},{10,9... | collective-permute-start | bytes 1572872 | tf_op jit(solution)/shard_map/ppermute | solution.py:56
  49.6 17.7 %collective-permute-start.3 = (bf16[1,2048,128]{2,1,0:T(8,128)(2,1)}, bf16[1,2048,128]{2,1,0:T(8,128)(2,1)S(1)}, u32[]{:S(2)}, u32[]{:S(2)}) collective-permute-start(bf16[1,2048,128]{2,1,0:T(8,128)(2,1)} %collective-permute-done.1), channel_id=1, source_target_pairs={{0,1},{1,2},{2,3},{3,4},{4,5},{5,6},{6,7},{7,8},{8,9},{9,10},{10,1... | collective-permute-start | bytes 1572872 | tf_op jit(solution)/shard_map/ppermute | solution.py:51
  52.4 19.7 %collective-permute-start.4 = (bf16[1,2048,128]{2,1,0:T(8,128)(2,1)S(1)}, bf16[1,2048,128]{2,1,0:T(8,128)(2,1)S(1)}, u32[]{:S(2)}, u32[]{:S(2)}) collective-permute-start(bf16[1,2048,128]{2,1,0:T(8,128)(2,1)S(1)} %collective-permute-done.2), channel_id=1, source_target_pairs={{0,15},{1,0},{2,1},{3,2},{4,3},{5,4},{6,5},{7,6},{8,7},{9,8},{10,9... | collective-permute-start | bytes 1572872 | tf_op jit(solution)/shard_map/ppermute | solution.py:56
  60.9 17.8 %collective-permute-start.20 = (bf16[1,2048,128]{2,1,0:T(8,128)(2,1)S(1)}, bf16[1,2048,128]{2,1,0:T(8,128)(2,1)S(1)}, u32[]{:S(2)}, u32[]{:S(2)}) collective-permute-start(bf16[1,2048,128]{2,1,0:T(8,128)(2,1)S(1)} %collective-permute-done.18), channel_id=1, source_target_pairs={{0,1},{1,2},{2,3},{3,4},{4,5},{5,6},{6,7},{7,8},{8,9},{9,10},{10,1... | collective-permute-start | bytes 1572872 | tf_op jit(solution)/shard_map/ppermute | solution.py:51
  67.3 15.9 %collective-permute-start.21 = (bf16[1,2048,128]{2,1,0:T(8,128)(2,1)S(1)}, bf16[1,2048,128]{2,1,0:T(8,128)(2,1)S(1)}, u32[]{:S(2)}, u32[]{:S(2)}) collective-permute-start(bf16[1,2048,128]{2,1,0:T(8,128)(2,1)S(1)} %collective-permute-done.19), channel_id=1, source_target_pairs={{0,15},{1,0},{2,1},{3,2},{4,3},{5,4},{6,5},{7,6},{8,7},{9,8},{10,9... | collective-permute-start | bytes 1572872 | tf_op jit(solution)/shard_map/ppermute | solution.py:56
  72.1 17.8 %collective-permute-start.5 = (bf16[1,2048,128]{2,1,0:T(8,128)(2,1)S(1)}, bf16[1,2048,128]{2,1,0:T(8,128)(2,1)S(1)}, u32[]{:S(2)}, u32[]{:S(2)}) collective-permute-start(bf16[1,2048,128]{2,1,0:T(8,128)(2,1)S(1)} %collective-permute-done.3), channel_id=1, source_target_pairs={{0,1},{1,2},{2,3},{3,4},{4,5},{5,6},{6,7},{7,8},{8,9},{9,10},{10,1... | collective-permute-start | bytes 1572872 | tf_op jit(solution)/shard_map/ppermute | solution.py:51
  78.7 15.4 %collective-permute-start.6 = (bf16[1,2048,128]{2,1,0:T(8,128)(2,1)S(1)}, bf16[1,2048,128]{2,1,0:T(8,128)(2,1)S(1)}, u32[]{:S(2)}, u32[]{:S(2)}) collective-permute-start(bf16[1,2048,128]{2,1,0:T(8,128)(2,1)S(1)} %collective-permute-done.4), channel_id=1, source_target_pairs={{0,15},{1,0},{2,1},{3,2},{4,3},{5,4},{6,5},{7,6},{8,7},{9,8},{10,9... | collective-permute-start | bytes 1572872 | tf_op jit(solution)/shard_map/ppermute | solution.py:56
  83.2 17.4 %collective-permute-start.22 = (bf16[1,2048,128]{2,1,0:T(8,128)(2,1)S(1)}, bf16[1,2048,128]{2,1,0:T(8,128)(2,1)S(1)}, u32[]{:S(2)}, u32[]{:S(2)}) collective-permute-start(bf16[1,2048,128]{2,1,0:T(8,128)(2,1)S(1)} %collective-permute-done.20), channel_id=1, source_target_pairs={{0,1},{1,2},{2,3},{3,4},{4,5},{5,6},{6,7},{7,8},{8,9},{9,10},{10,1... | collective-permute-start | bytes 1572872 | tf_op jit(solution)/shard_map/ppermute | solution.py:51
  89.9 15.1 %collective-permute-start.23 = (bf16[1,2048,128]{2,1,0:T(8,128)(2,1)S(1)}, bf16[1,2048,128]{2,1,0:T(8,128)(2,1)S(1)}, u32[]{:S(2)}, u32[]{:S(2)}) collective-permute-start(bf16[1,2048,128]{2,1,0:T(8,128)(2,1)S(1)} %collective-permute-done.21), channel_id=1, source_target_pairs={{0,15},{1,0},{2,1},{3,2},{4,3},{5,4},{6,5},{7,6},{8,7},{9,8},{10,9... | collective-permute-start | bytes 1572872 | tf_op jit(solution)/shard_map/ppermute | solution.py:56
  94.1 17.5 %collective-permute-start.7 = (bf16[1,2048,128]{2,1,0:T(8,128)(2,1)S(1)}, bf16[1,2048,128]{2,1,0:T(8,128)(2,1)S(1)}, u32[]{:S(2)}, u32[]{:S(2)}) collective-permute-start(bf16[1,2048,128]{2,1,0:T(8,128)(2,1)S(1)} %collective-permute-done.5), channel_id=1, source_target_pairs={{0,1},{1,2},{2,3},{3,4},{4,5},{5,6},{6,7},{7,8},{8,9},{9,10},{10,1... | collective-permute-start | bytes 1572872 | tf_op jit(solution)/shard_map/ppermute | solution.py:51
  100.7 15.1 %collective-permute-start.8 = (bf16[1,2048,128]{2,1,0:T(8,128)(2,1)S(1)}, bf16[1,2048,128]{2,1,0:T(8,128)(2,1)S(1)}, u32[]{:S(2)}, u32[]{:S(2)}) collective-permute-start(bf16[1,2048,128]{2,1,0:T(8,128)(2,1)S(1)} %collective-permute-done.6), channel_id=1, source_target_pairs={{0,15},{1,0},{2,1},{3,2},{4,3},{5,4},{6,5},{7,6},{8,7},{9,8},{10,9... | collective-permute-start | bytes 1572872 | tf_op jit(solution)/shard_map/ppermute | solution.py:56
  105.0 17.5 %collective-permute-start.24 = (bf16[1,2048,128]{2,1,0:T(8,128)(2,1)S(1)}, bf16[1,2048,128]{2,1,0:T(8,128)(2,1)S(1)}, u32[]{:S(2)}, u32[]{:S(2)}) collective-permute-start(bf16[1,2048,128]{2,1,0:T(8,128)(2,1)S(1)} %collective-permute-done.22), channel_id=1, source_target_pairs={{0,1},{1,2},{2,3},{3,4},{4,5},{5,6},{6,7},{7,8},{8,9},{9,10},{10,1... | collective-permute-start | bytes 1572872 | tf_op jit(solution)/shard_map/ppermute | solution.py:51
  111.6 15.2 %collective-permute-start.25 = (bf16[1,2048,128]{2,1,0:T(8,128)(2,1)S(1)}, bf16[1,2048,128]{2,1,0:T(8,128)(2,1)S(1)}, u32[]{:S(2)}, u32[]{:S(2)}) collective-permute-start(bf16[1,2048,128]{2,1,0:T(8,128)(2,1)S(1)} %collective-permute-done.23), channel_id=1, source_target_pairs={{0,15},{1,0},{2,1},{3,2},{4,3},{5,4},{6,5},{7,6},{8,7},{9,8},{10,9... | collective-permute-start | bytes 1572872 | tf_op jit(solution)/shard_map/ppermute | solution.py:56
  115.8 17.6 %collective-permute-start.9 = (bf16[1,2048,128]{2,1,0:T(8,128)(2,1)S(1)}, bf16[1,2048,128]{2,1,0:T(8,128)(2,1)S(1)}, u32[]{:S(2)}, u32[]{:S(2)}) collective-permute-start(bf16[1,2048,128]{2,1,0:T(8,128)(2,1)S(1)} %collective-permute-done.7), channel_id=1, source_target_pairs={{0,1},{1,2},{2,3},{3,4},{4,5},{5,6},{6,7},{7,8},{8,9},{9,10},{10,1... | collective-permute-start | bytes 1572872 | tf_op jit(solution)/shard_map/ppermute | solution.py:51
  122.4 15.1 %collective-permute-start.10 = (bf16[1,2048,128]{2,1,0:T(8,128)(2,1)S(1)}, bf16[1,2048,128]{2,1,0:T(8,128)(2,1)S(1)}, u32[]{:S(2)}, u32[]{:S(2)}) collective-permute-start(bf16[1,2048,128]{2,1,0:T(8,128)(2,1)S(1)} %collective-permute-done.8), channel_id=1, source_target_pairs={{0,15},{1,0},{2,1},{3,2},{4,3},{5,4},{6,5},{7,6},{8,7},{9,8},{10,9... | collective-permute-start | bytes 1572872 | tf_op jit(solution)/shard_map/ppermute | solution.py:56
  126.8 17.4 %collective-permute-start.26 = (bf16[1,2048,128]{2,1,0:T(8,128)(2,1)S(1)}, bf16[1,2048,128]{2,1,0:T(8,128)(2,1)S(1)}, u32[]{:S(2)}, u32[]{:S(2)}) collective-permute-start(bf16[1,2048,128]{2,1,0:T(8,128)(2,1)S(1)} %collective-permute-done.24), channel_id=1, source_target_pairs={{0,1},{1,2},{2,3},{3,4},{4,5},{5,6},{6,7},{7,8},{8,9},{9,10},{10,1... | collective-permute-start | bytes 1572872 | tf_op jit(solution)/shard_map/ppermute | solution.py:51
  133.4 15.2 %collective-permute-start.27 = (bf16[1,2048,128]{2,1,0:T(8,128)(2,1)S(1)}, bf16[1,2048,128]{2,1,0:T(8,128)(2,1)S(1)}, u32[]{:S(2)}, u32[]{:S(2)}) collective-permute-start(bf16[1,2048,128]{2,1,0:T(8,128)(2,1)S(1)} %collective-permute-done.25), channel_id=1, source_target_pairs={{0,15},{1,0},{2,1},{3,2},{4,3},{5,4},{6,5},{7,6},{8,7},{9,8},{10,9... | collective-permute-start | bytes 1572872 | tf_op jit(solution)/shard_map/ppermute | solution.py:56
  137.6 17.6 %collective-permute-start.11 = (bf16[1,2048,128]{2,1,0:T(8,128)(2,1)S(1)}, bf16[1,2048,128]{2,1,0:T(8,128)(2,1)S(1)}, u32[]{:S(2)}, u32[]{:S(2)}) collective-permute-start(bf16[1,2048,128]{2,1,0:T(8,128)(2,1)S(1)} %collective-permute-done.9), channel_id=1, source_target_pairs={{0,1},{1,2},{2,3},{3,4},{4,5},{5,6},{6,7},{7,8},{8,9},{9,10},{10,1... | collective-permute-start | bytes 1572872 | tf_op jit(solution)/shard_map/ppermute | solution.py:51
  144.2 15.1 %collective-permute-start.12 = (bf16[1,2048,128]{2,1,0:T(8,128)(2,1)S(1)}, bf16[1,2048,128]{2,1,0:T(8,128)(2,1)S(1)}, u32[]{:S(2)}, u32[]{:S(2)}) collective-permute-start(bf16[1,2048,128]{2,1,0:T(8,128)(2,1)S(1)} %collective-permute-done.10), channel_id=1, source_target_pairs={{0,15},{1,0},{2,1},{3,2},{4,3},{5,4},{6,5},{7,6},{8,7},{9,8},{10,9... | collective-permute-start | bytes 1572872 | tf_op jit(solution)/shard_map/ppermute | solution.py:56
  148.6 17.4 %collective-permute-start.28 = (bf16[1,2048,128]{2,1,0:T(8,128)(2,1)S(1)}, bf16[1,2048,128]{2,1,0:T(8,128)(2,1)S(1)}, u32[]{:S(2)}, u32[]{:S(2)}) collective-permute-start(bf16[1,2048,128]{2,1,0:T(8,128)(2,1)S(1)} %collective-permute-done.26), channel_id=1, source_target_pairs={{0,1},{1,2},{2,3},{3,4},{4,5},{5,6},{6,7},{7,8},{8,9},{9,10},{10,1... | collective-permute-start | bytes 1572872 | tf_op jit(solution)/shard_map/ppermute | solution.py:51
  155.1 15.1 %collective-permute-start.29 = (bf16[1,2048,128]{2,1,0:T(8,128)(2,1)S(1)}, bf16[1,2048,128]{2,1,0:T(8,128)(2,1)}, u32[]{:S(2)}, u32[]{:S(2)}) collective-permute-start(bf16[1,2048,128]{2,1,0:T(8,128)(2,1)S(1)} %collective-permute-done.27), channel_id=1, source_target_pairs={{0,15},{1,0},{2,1},{3,2},{4,3},{5,4},{6,5},{7,6},{8,7},{9,8},{10,9... | collective-permute-start | bytes 1572872 | tf_op jit(solution)/shard_map/ppermute | solution.py:56
  159.3 17.6 %collective-permute-start.13 = (bf16[1,2048,128]{2,1,0:T(8,128)(2,1)S(1)}, bf16[1,2048,128]{2,1,0:T(8,128)(2,1)S(1)}, u32[]{:S(2)}, u32[]{:S(2)}) collective-permute-start(bf16[1,2048,128]{2,1,0:T(8,128)(2,1)S(1)} %collective-permute-done.11), channel_id=1, source_target_pairs={{0,1},{1,2},{2,3},{3,4},{4,5},{5,6},{6,7},{7,8},{8,9},{9,10},{10,1... | collective-permute-start | bytes 1572872 | tf_op jit(solution)/shard_map/ppermute | solution.py:51
  166.0 25.7 %collective-permute-start.14 = (bf16[1,2048,128]{2,1,0:T(8,128)(2,1)S(1)}, bf16[1,2048,128]{2,1,0:T(8,128)(2,1)S(1)}, u32[]{:S(2)}, u32[]{:S(2)}) collective-permute-start(bf16[1,2048,128]{2,1,0:T(8,128)(2,1)S(1)} %collective-permute-done.12), channel_id=1, source_target_pairs={{0,15},{1,0},{2,1},{3,2},{4,3},{5,4},{6,5},{7,6},{8,7},{9,8},{10,9... | collective-permute-start | bytes 1572872 | tf_op jit(solution)/shard_map/ppermute | solution.py:56
  170.3 86.0 %copy-start = (f32[1,2048,128]{2,1,0:T(8,128)S(1)}, f32[1,2048,128]{2,1,0:T(8,128)}, u32[]{:S(2)}) copy-start(f32[1,2048,128]{2,1,0:T(8,128)} %param.5) | copy-start | bytes 3145732
  170.3 17.5 %collective-permute-start.30 = (bf16[1,2048,128]{2,1,0:T(8,128)(2,1)S(1)}, bf16[1,2048,128]{2,1,0:T(8,128)(2,1)}, u32[]{:S(2)}, u32[]{:S(2)}) collective-permute-start(bf16[1,2048,128]{2,1,0:T(8,128)(2,1)S(1)} %collective-permute-done.28), channel_id=1, source_target_pairs={{0,1},{1,2},{2,3},{3,4},{4,5},{5,6},{6,7},{7,8},{8,9},{9,10},{10,1... | collective-permute-start | bytes 1572872 | tf_op jit(solution)/shard_map/ppermute | solution.py:51
  176.9 87.3 %collective-permute-start.31 = (bf16[1,2048,128]{2,1,0:T(8,128)(2,1)}, bf16[1,2048,128]{2,1,0:T(8,128)(2,1)}, u32[]{:S(2)}, u32[]{:S(2)}) collective-permute-start(bf16[1,2048,128]{2,1,0:T(8,128)(2,1)} %collective-permute-done.29), channel_id=1, source_target_pairs={{0,15},{1,0},{2,1},{3,2},{4,3},{5,4},{6,5},{7,6},{8,7},{9,8},{10,9... | collective-permute-start | bytes 1572872 | tf_op jit(solution)/shard_map/ppermute | solution.py:56
  187.7 13.2 %collective-permute-start.15 = (bf16[1,2048,128]{2,1,0:T(8,128)(2,1)S(1)}, bf16[1,2048,128]{2,1,0:T(8,128)(2,1)S(1)}, u32[]{:S(2)}, u32[]{:S(2)}) collective-permute-start(bf16[1,2048,128]{2,1,0:T(8,128)(2,1)S(1)} %collective-permute-done.13), channel_id=1, source_target_pairs={{0,1},{1,2},{2,3},{3,4},{4,5},{5,6},{6,7},{7,8},{8,9},{9,10},{10,1... | collective-permute-start | bytes 1572872 | tf_op jit(solution)/shard_map/ppermute | solution.py:51
  191.6 74.5 %collective-permute-start.32 = (bf16[1,2048,128]{2,1,0:T(8,128)(2,1)}, bf16[1,2048,128]{2,1,0:T(8,128)(2,1)}, u32[]{:S(2)}, u32[]{:S(2)}) collective-permute-start(bf16[1,2048,128]{2,1,0:T(8,128)(2,1)} %collective-permute-done.30), channel_id=1, source_target_pairs={{0,1},{1,2},{2,3},{3,4},{4,5},{5,6},{6,7},{7,8},{8,9},{9,10},{10,1... | collective-permute-start | bytes 1572872 | tf_op jit(solution)/shard_map/ppermute | solution.py:51
  207.7 0.8 copy-start.1
  262.9 14.0 %collective-permute-start.33 = (bf16[2048,128]{1,0:T(8,128)(2,1)}, bf16[2048,128]{1,0:T(8,128)(2,1)S(1)}, u32[]{:S(2)}, u32[]{:S(2)}) collective-permute-start(bf16[2048,128]{1,0:T(8,128)(2,1)} %get-tuple-element.5), channel_id=1, source_target_pairs={{32,0},{48,16},{64,32},{80,48},{96,64},{112,80},{128,96},{144,112}... | collective-permute-start | bytes 1572872 | tf_op jit(solution)/shard_map/ppermute | solution.py:23
  268.1 85.4 %collective-permute-start.17 = (bf16[2048,128]{1,0:T(8,128)(2,1)}, bf16[2048,128]{1,0:T(8,128)(2,1)S(1)}, u32[]{:S(2)}, u32[]{:S(2)}) collective-permute-start(bf16[2048,128]{1,0:T(8,128)(2,1)} %get-tuple-element.5), channel_id=1, source_target_pairs={{0,32},{16,48},{32,64},{48,80},{64,96},{80,112},{96,128},{112,144}... | collective-permute-start | bytes 1572872 | tf_op jit(solution)/shard_map/ppermute | solution.py:23
Sparse Core Ops, SparseCore 0:
  10.3 245.8 all-gather.2
  259.2 94.1 all-gather.4
